TPU v7x, 32 devices: a whole 2x2x4 slice. The times are simulated.
32 devices in a mesh: tm: 4 (over y, x), gx: 8 (over z, core).
Axes of the slice: x: 2, y: 2, z: 4, core: 2. Of those that a mesh axis runs over, the one named last changes fastest.
Arguments:
- state: float32 [8, 32, 256, 128], P('tm', 'gx'), may hold values from -3 to 3
- start_field: float32 [32, 256, 128], P('gx'), may hold values from -3 to 3
- diffusivity: float32 [32, 256, 128], P('gx'), may hold values from 0.3 to 3
- time_weights: float32 [8], P('tm'), may hold values from 0.4 to 1
- shift_real: float32 [8], replicated, may hold values from 0.5 to 2, as said below
- shift_imag: float32 [8], replicated, may hold values from -1 to 1, as said below
Outputs:
- new_state: float32 [8, 32, 256, 128], P('tm', 'gx')
Inputs may be any that keep to these rules, and one draw needn't show every extreme that they name: `shift_real`: shift_real_k = shift_real_(8 - k) for k = 1 .. 7. `shift_imag`: shift_imag_0 = shift_imag_(4) = 0 and shift_imag_k = - shift_imag_(8 - k), so the eigenvalues come in conjugate pairs.
All inputs are finite; a program needn't handle non-finite values.
Results may differ from a plain program's by a relative error of at most 0.0003.
Values sent between devices are 32-bit elements; how exact they have to be, the bound alone decides.
No kernel may reach another device: no remote copies, remote signals or barrier semaphores. Data moves between devices by JAX's collectives and lax.ppermute only.
A program may use at most 64 MiB of HBM per device.

v0:
```python
import math
import jax
import jax.numpy as jnp
from jax import lax
from jax.sharding import PartitionSpec as P

SWEEPS = 12
cheb_centre = 1.0
cheb_half = 0.7


def padded_2(block, sides, width):
    for axis, dim in sides:
        count = lax.axis_size(axis)
        forward = [(i, i + 1) for i in range(count - 1)]
        backward = [(target, source) for source, target in forward]
        low = lax.ppermute(
            lax.slice_in_dim(block, block.shape[dim] - width, None, axis=dim), axis, forward
        )
        high = lax.ppermute(lax.slice_in_dim(block, 0, width, axis=dim), axis, backward)
        block = jnp.concatenate([low, block, high], axis=dim)
    return block


def shifted(value, axis, steps):
    count = lax.axis_size(axis)
    initial, last = (max(0, -steps), min(count, count - steps))
    return lax.ppermute(value, axis, [(source, source + steps) for source in range(initial, last)])


def along(core, axis, lower):
    length = core.shape[axis]
    zeros = jnp.zeros_like(lax.slice_in_dim(core, 0, 1, axis=axis))
    if lower:
        return jnp.concatenate([zeros, lax.slice_in_dim(core, 0, length - 1, axis=axis)], axis)
    return jnp.concatenate([lax.slice_in_dim(core, 1, length, axis=axis), zeros], axis)


def six_near(padded):
    core = padded[..., 1:-1, :, :]
    rank = core.ndim
    return (
        core,
        (
            padded[..., :-2, :, :],
            padded[..., 2:, :, :],
            along(core, rank - 2, True),
            along(core, rank - 2, False),
            along(core, rank - 1, True),
            along(core, rank - 1, False),
        ),
    )


def operate(padded, faces, diag_sum):
    core, near = six_near(padded)
    total = faces[0] * near[0]
    for which in range(1, 6):
        total = total + faces[which] * near[which]
    return diag_sum * core - total


def time_matrix(total_steps, sign):
    index = lax.iota(jnp.int32, total_steps)
    product = index[:, None] * index[None, :] % total_steps
    angle = product.astype(jnp.float32) * (2.0 * math.pi / total_steps)
    cosine = jnp.cos(angle)
    sine = jnp.sin(angle) * sign
    matrix = jnp.stack([jnp.stack([cosine, sine], -1), jnp.stack([-sine, cosine], -1)], 1)
    return matrix.reshape((2 * total_steps, 2 * total_steps))


def apply_time(field, sign):
    total_steps = field.shape[0]
    flat = field.reshape((2 * total_steps, -1))
    mixed = jnp.dot(
        time_matrix(total_steps, sign),
        flat,
        precision=lax.Precision.HIGHEST,
        preferred_element_type=jnp.float32,
    )
    return mixed.reshape(field.shape)


def forward_time(field):
    return apply_time(field, 1.0)


def inverse_time(field):
    return apply_time(field, -1.0)


def shards(state, start_field, diffusivity, time_weights, shift_real, shift_imag):
    local_steps = state.shape[0]
    total_steps = local_steps * lax.axis_size("tm")
    device = lax.axis_index("tm")
    stacked = jnp.concatenate([diffusivity[None], state], 0)
    padded = padded_2(stacked, (("gx", 1),), 1)
    kappa, near = six_near(padded[0])
    faces = [0.5 * (kappa + other) for other in near]
    diag_sum = faces[0]
    for which in range(1, 6):
        diag_sum = diag_sum + faces[which]
    carried = shifted(state[local_steps - 1], "tm", 1)
    first_prior = jnp.where(device == 0, start_field, carried)
    prior = jnp.concatenate([first_prior[None], state[: local_steps - 1]], 0)
    applied = operate(padded[1:], faces, diag_sum)
    residual = prior - state - (applied + state * state * state - state)
    weighted = time_weights[:, None, None, None] * residual
    field = jnp.stack([weighted, jnp.zeros_like(weighted)], 1)
    local_index = device * local_steps + lax.iota(jnp.int32, local_steps)
    spectral = forward_time(lax.all_to_all(field, "tm", split_axis=3, concat_axis=0, tiled=True))
    spectral = lax.all_to_all(spectral, "tm", split_axis=0, concat_axis=3, tiled=True)
    chooser = (local_index[:, None] == lax.iota(jnp.int32, total_steps)[None, :]).astype(
        jnp.float32
    )
    mode_real = jnp.dot(
        chooser, shift_real, precision=lax.Precision.HIGHEST, preferred_element_type=jnp.float32
    ).reshape((-1, 1, 1, 1))
    mode_imag = jnp.dot(
        chooser, shift_imag, precision=lax.Precision.HIGHEST, preferred_element_type=jnp.float32
    ).reshape((-1, 1, 1, 1))
    denom_real = mode_real + diag_sum
    magnitude = denom_real * denom_real + mode_imag * mode_imag
    inverse_real = denom_real / magnitude
    inverse_imag = -mode_imag / magnitude
    source_real = spectral[:, 0]
    source_imag = spectral[:, 1]
    solution = jnp.stack(
        [
            source_real * inverse_real - source_imag * inverse_imag,
            source_real * inverse_imag + source_imag * inverse_real,
        ],
        1,
    )

    def sweep(turn, current):
        omega = 1.0 / (
            cheb_centre
            + cheb_half * jnp.cos(math.pi * (2.0 * turn.astype(jnp.float32) + 1.0) / (2.0 * SWEEPS))
        )
        extended = padded_2(current, (("gx", 2),), 1)
        image = operate(extended, faces, diag_sum)
        answer_real = current[:, 0]
        answer_imag = current[:, 1]
        misfit_real = source_real - (
            mode_real * answer_real - mode_imag * answer_imag + image[:, 0]
        )
        misfit_imag = source_imag - (
            mode_real * answer_imag + mode_imag * answer_real + image[:, 1]
        )
        return jnp.stack(
            [
                answer_real + omega * (misfit_real * inverse_real - misfit_imag * inverse_imag),
                answer_imag + omega * (misfit_real * inverse_imag + misfit_imag * inverse_real),
            ],
            1,
        )

    solution = lax.fori_loop(0, SWEEPS, sweep, solution)
    back = inverse_time(lax.all_to_all(solution, "tm", split_axis=3, concat_axis=0, tiled=True))
    back = lax.all_to_all(back, "tm", split_axis=0, concat_axis=3, tiled=True)
    delta = back[:, 0] / (total_steps * time_weights[:, None, None, None])
    return state + delta


def solution(mesh):
    in_specs = (
        P("tm", "gx", None, None),
        P("gx", None, None),
        P("gx", None, None),
        P("tm"),
        P(),
        P(),
    )
    out_specs = P("tm", "gx", None, None)
    return jax.shard_map(shards, mesh=mesh, in_specs=in_specs, out_specs=out_specs, check_vma=False)
```

profile of v0, /device:TPU:0, one launch (start us, length us, event | category | flops | bytes accessed | tf_op | source)
XLA Modules:
  0.0 402.5 jit_solution(8984971837982444184)
XLA Ops:
  2.4 5.7 %collective-permute-start.2 = (f32[4,256,128]{2,0,1:T(4,128)}, f32[4,256,128]{2,0,1:T(4,128)}, u32[]{:S(2)}, u32[]{:S(2)}) collective-permute-start(f32[4,256,128]{2,0,1:T(4,128)} %bitcast.138), channel_id=1, source_target_pairs={{0,8},{8,16},{16,24},{1,9},{9,17},{17,25},{2,10},{10,18},{18,26},{... | collective-permute-start | bytes 1572872 | tf_op jit(solution)/shard_map/ppermute | solution.py:28
  9.1 1.6 pad_maximum_fusion.11
  16.9 2.3 copy.153
  19.1 2.2 copy.154
  24.4 2.0 multiply_bitcast_fusion.1
  26.4 3.4 add_add_fusion
  30.3 1.6 copy-done.23
  31.9 3.9 fusion.40
  35.8 1.7 stack.76
  37.5 3.8 all-to-all-start
  41.7 24.5 %all-to-all-done = f32[2,2,4,256,128]{4,2,0,1,3:T(4,128)S(1)} async-done(((f32[2,2,4,256,128]{4,2,0,1,3:T(4,128)}), f32[2,2,4,256,128]{4,2,0,1,3:T(4,128)S(1)}, u32[]{:S(2)}, u32[]{:S(2)}) %all-to-all-start) | async-done | bytes 2097184 | tf_op jit(solution)/shard_map/all_to_all | solution.py:112
  66.3 2.0 copy.162
  68.3 1.7 reshape.221
  70.5 2.8 fusion.30
  73.3 1.7 copy.107
  75.0 3.7 all-to-all-start.1
  84.7 20.2 %all-to-all-done.1 = f32[8,2,4,64,128]{4,3,2,1,0:T(8,128)S(1)} async-done(((f32[8,2,4,64,128]{4,3,2,1,0:T(8,128)}), f32[8,2,4,64,128]{4,3,2,1,0:T(8,128)S(1)}, u32[]{:S(2)}, u32[]{:S(2)}) %all-to-all-start.1) | async-done | bytes 2097184 | tf_op jit(solution)/shard_map/all_to_all | solution.py:113
  105.2 1.9 multiply_subtract_fusion
  107.4 222.7 %while.17 = (s32[]{:T(128)}, f32[2,2,4,256,128]{4,3,2,1,0:T(8,128)S(1)}, f32[2,4,256,128]{3,2,1,0:T(8,128)}, f32[2,1,1,1]{0,3,2,1:T(1,128)S(1)}, f32[2,1,1,1]{0,...) while((s32[]{:T(128)}, ...), condition=%wide.region_1.2_spmd.clone.clone, body=%wide.region_0.1_spmd.clone.clone.sunk | while | flops 16252937 | bytes 94683824 | solution.py:160
  109.7 3.8 collective-permute-start.1
  113.6 2.4 fusion.95
  119.0 3.3 fusion.96
  126.2 5.9 %collective-permute-start.1 = (f32[2,2,1,256,128]{4,3,2,1,0:T(8,128)}, f32[2,2,1,256,128]{4,3,2,1,0:T(8,128)}, u32[]{:S(2)}, u32[]{:S(2)}) collective-permute-start(f32[2,2,1,256,128]{4,3,2,1,0:T(8,128)} %get-tuple-element.695), channel_id=1, source_target_pairs={{0,1},{1,2},{2,3},{3,4},{4,5},{5,6},{6,7},{8,9},{9,10},{10,11},{11... | collective-permute-start | bytes 1572872 | tf_op jit(solution)/shard_map/while/body/eval_jaxpr/ppermute | solution.py:17
  132.2 2.4 fusion.95
  137.6 3.3 fusion.96
  144.8 6.1 %collective-permute-start.1 = (f32[2,2,1,256,128]{4,3,2,1,0:T(8,128)}, f32[2,2,1,256,128]{4,3,2,1,0:T(8,128)}, u32[]{:S(2)}, u32[]{:S(2)}) collective-permute-start(f32[2,2,1,256,128]{4,3,2,1,0:T(8,128)} %get-tuple-element.695), channel_id=1, source_target_pairs={{0,1},{1,2},{2,3},{3,4},{4,5},{5,6},{6,7},{8,9},{9,10},{10,11},{11... | collective-permute-start | bytes 1572872 | tf_op jit(solution)/shard_map/while/body/eval_jaxpr/ppermute | solution.py:17
  150.9 2.4 fusion.95
  156.3 3.3 fusion.96
  163.6 6.1 %collective-permute-start.1 = (f32[2,2,1,256,128]{4,3,2,1,0:T(8,128)}, f32[2,2,1,256,128]{4,3,2,1,0:T(8,128)}, u32[]{:S(2)}, u32[]{:S(2)}) collective-permute-start(f32[2,2,1,256,128]{4,3,2,1,0:T(8,128)} %get-tuple-element.695), channel_id=1, source_target_pairs={{0,1},{1,2},{2,3},{3,4},{4,5},{5,6},{6,7},{8,9},{9,10},{10,11},{11... | collective-permute-start | bytes 1572872 | tf_op jit(solution)/shard_map/while/body/eval_jaxpr/ppermute | solution.py:17
  169.7 2.4 fusion.95
  175.1 3.3 fusion.96
  182.3 6.1 %collective-permute-start.1 = (f32[2,2,1,256,128]{4,3,2,1,0:T(8,128)}, f32[2,2,1,256,128]{4,3,2,1,0:T(8,128)}, u32[]{:S(2)}, u32[]{:S(2)}) collective-permute-start(f32[2,2,1,256,128]{4,3,2,1,0:T(8,128)} %get-tuple-element.695), channel_id=1, source_target_pairs={{0,1},{1,2},{2,3},{3,4},{4,5},{5,6},{6,7},{8,9},{9,10},{10,11},{11... | collective-permute-start | bytes 1572872 | tf_op jit(solution)/shard_map/while/body/eval_jaxpr/ppermute | solution.py:17
  188.4 2.4 fusion.95
  193.9 3.3 fusion.96
  201.1 6.1 %collective-permute-start.1 = (f32[2,2,1,256,128]{4,3,2,1,0:T(8,128)}, f32[2,2,1,256,128]{4,3,2,1,0:T(8,128)}, u32[]{:S(2)}, u32[]{:S(2)}) collective-permute-start(f32[2,2,1,256,128]{4,3,2,1,0:T(8,128)} %get-tuple-element.695), channel_id=1, source_target_pairs={{0,1},{1,2},{2,3},{3,4},{4,5},{5,6},{6,7},{8,9},{9,10},{10,11},{11... | collective-permute-start | bytes 1572872 | tf_op jit(solution)/shard_map/while/body/eval_jaxpr/ppermute | solution.py:17
  207.2 2.4 fusion.95
  212.6 3.3 fusion.96
  219.9 6.1 %collective-permute-start.1 = (f32[2,2,1,256,128]{4,3,2,1,0:T(8,128)}, f32[2,2,1,256,128]{4,3,2,1,0:T(8,128)}, u32[]{:S(2)}, u32[]{:S(2)}) collective-permute-start(f32[2,2,1,256,128]{4,3,2,1,0:T(8,128)} %get-tuple-element.695), channel_id=1, source_target_pairs={{0,1},{1,2},{2,3},{3,4},{4,5},{5,6},{6,7},{8,9},{9,10},{10,11},{11... | collective-permute-start | bytes 1572872 | tf_op jit(solution)/shard_map/while/body/eval_jaxpr/ppermute | solution.py:17
  226.0 2.4 fusion.95
  231.4 3.3 fusion.96
  238.6 6.1 %collective-permute-start.1 = (f32[2,2,1,256,128]{4,3,2,1,0:T(8,128)}, f32[2,2,1,256,128]{4,3,2,1,0:T(8,128)}, u32[]{:S(2)}, u32[]{:S(2)}) collective-permute-start(f32[2,2,1,256,128]{4,3,2,1,0:T(8,128)} %get-tuple-element.695), channel_id=1, source_target_pairs={{0,1},{1,2},{2,3},{3,4},{4,5},{5,6},{6,7},{8,9},{9,10},{10,11},{11... | collective-permute-start | bytes 1572872 | tf_op jit(solution)/shard_map/while/body/eval_jaxpr/ppermute | solution.py:17
  244.7 2.4 fusion.95
  250.2 3.3 fusion.96
  257.4 6.1 %collective-permute-start.1 = (f32[2,2,1,256,128]{4,3,2,1,0:T(8,128)}, f32[2,2,1,256,128]{4,3,2,1,0:T(8,128)}, u32[]{:S(2)}, u32[]{:S(2)}) collective-permute-start(f32[2,2,1,256,128]{4,3,2,1,0:T(8,128)} %get-tuple-element.695), channel_id=1, source_target_pairs={{0,1},{1,2},{2,3},{3,4},{4,5},{5,6},{6,7},{8,9},{9,10},{10,11},{11... | collective-permute-start | bytes 1572872 | tf_op jit(solution)/shard_map/while/body/eval_jaxpr/ppermute | solution.py:17
  263.5 2.4 fusion.95
  268.9 3.3 fusion.96
  276.1 6.1 %collective-permute-start.1 = (f32[2,2,1,256,128]{4,3,2,1,0:T(8,128)}, f32[2,2,1,256,128]{4,3,2,1,0:T(8,128)}, u32[]{:S(2)}, u32[]{:S(2)}) collective-permute-start(f32[2,2,1,256,128]{4,3,2,1,0:T(8,128)} %get-tuple-element.695), channel_id=1, source_target_pairs={{0,1},{1,2},{2,3},{3,4},{4,5},{5,6},{6,7},{8,9},{9,10},{10,11},{11... | collective-permute-start | bytes 1572872 | tf_op jit(solution)/shard_map/while/body/eval_jaxpr/ppermute | solution.py:17
  282.3 2.4 fusion.95
  287.7 3.3 fusion.96
  294.9 6.1 %collective-permute-start.1 = (f32[2,2,1,256,128]{4,3,2,1,0:T(8,128)}, f32[2,2,1,256,128]{4,3,2,1,0:T(8,128)}, u32[]{:S(2)}, u32[]{:S(2)}) collective-permute-start(f32[2,2,1,256,128]{4,3,2,1,0:T(8,128)} %get-tuple-element.695), channel_id=1, source_target_pairs={{0,1},{1,2},{2,3},{3,4},{4,5},{5,6},{6,7},{8,9},{9,10},{10,11},{11... | collective-permute-start | bytes 1572872 | tf_op jit(solution)/shard_map/while/body/eval_jaxpr/ppermute | solution.py:17
  301.0 2.4 fusion.95
  306.4 3.3 fusion.96
  313.7 6.1 %collective-permute-start.1 = (f32[2,2,1,256,128]{4,3,2,1,0:T(8,128)}, f32[2,2,1,256,128]{4,3,2,1,0:T(8,128)}, u32[]{:S(2)}, u32[]{:S(2)}) collective-permute-start(f32[2,2,1,256,128]{4,3,2,1,0:T(8,128)} %get-tuple-element.695), channel_id=1, source_target_pairs={{0,1},{1,2},{2,3},{3,4},{4,5},{5,6},{6,7},{8,9},{9,10},{10,11},{11... | collective-permute-start | bytes 1572872 | tf_op jit(solution)/shard_map/while/body/eval_jaxpr/ppermute | solution.py:17
  319.8 2.4 fusion.95
  325.2 3.3 fusion.96
  330.1 2.7 copy.118
  332.8 3.8 all-to-all-start.2
  336.9 24.7 %all-to-all-done.2 = f32[2,2,4,256,128]{4,2,1,0,3:T(4,128)S(1)} async-done(((f32[2,2,4,256,128]{4,2,1,0,3:T(4,128)}), f32[2,2,4,256,128]{4,2,1,0,3:T(4,128)S(1)}, u32[]{:S(2)}, u32[]{:S(2)}) %all-to-all-start.2) | async-done | bytes 2097184 | tf_op jit(solution)/shard_map/all_to_all | solution.py:161
  361.6 2.0 copy.161
  363.6 1.7 reshape.224
  365.7 2.8 fusion.28
  368.6 1.7 copy.121
  370.3 3.6 all-to-all-start.3
  373.9 26.1 %all-to-all-done.3 = f32[8,2,4,64,128]{4,3,2,1,0:T(8,128)S(1)} async-done(((f32[8,2,4,64,128]{4,3,2,1,0:T(8,128)}), f32[8,2,4,64,128]{4,3,2,1,0:T(8,128)S(1)}, u32[]{:S(2)}, u32[]{:S(2)}) %all-to-all-start.3) | async-done | bytes 2097184 | tf_op jit(solution)/shard_map/all_to_all | solution.py:162
  (409 shorter events, 103.5 us)
Async XLA Ops:
  0.0 79.0 %copy-start = (f32[8]{0:T(128)S(1)}, f32[8]{0:T(128)}, u32[]{:S(2)}) copy-start(f32[8]{0:T(128)} %param.13) | copy-start | bytes 100
  0.0 8.0 %copy-start.12 = (f32[2,4,256,128]{3,2,1,0:T(8,128)S(1)}, f32[2,4,256,128]{3,2,1,0:T(8,128)}, u32[]{:S(2)}) copy-start(f32[2,4,256,128]{3,2,1,0:T(8,128)} %param.8) | copy-start | bytes 3145732
  0.0 8.7 %copy-start.6 = (f32[4,256,128]{2,1,0:T(8,128)S(1)}, f32[4,256,128]{2,1,0:T(8,128)}, u32[]{:S(2)}) copy-start(f32[4,256,128]{2,1,0:T(8,128)} %param.10) | copy-start | bytes 1572868
  2.4 27.5 %collective-permute-start.2 = (f32[4,256,128]{2,0,1:T(4,128)}, f32[4,256,128]{2,0,1:T(4,128)}, u32[]{:S(2)}, u32[]{:S(2)}) collective-permute-start(f32[4,256,128]{2,0,1:T(4,128)} %bitcast.138), channel_id=1, source_target_pairs={{0,8},{8,16},{16,24},{1,9},{9,17},{17,25},{2,10},{10,18},{18,26},{... | collective-permute-start | bytes 1572872 | tf_op jit(solution)/shard_map/ppermute | solution.py:28
  10.6 13.7 %collective-permute-start.3 = (f32[3,1,256,128]{3,1,0,2:T(1,128)}, f32[3,1,256,128]{3,1,0,2:T(1,128)S(1)}, u32[]{:S(2)}, u32[]{:S(2)}) collective-permute-start(f32[3,1,256,128]{3,1,0,2:T(1,128)} %get-tuple-element.566), channel_id=1, source_target_pairs={{0,1},{1,2},{2,3},{3,4},{4,5},{5,6},{6,7},{8,9},{9,10},{10,11},{11... | collective-permute-start | bytes 1179656 | tf_op jit(solution)/shard_map/ppermute | solution.py:17
  12.1 12.2 %collective-permute-start.4 = (f32[3,1,256,128]{3,1,0,2:T(1,128)}, f32[3,1,256,128]{3,1,0,2:T(1,128)}, u32[]{:S(2)}, u32[]{:S(2)}) collective-permute-start(f32[3,1,256,128]{3,1,0,2:T(1,128)} %get-tuple-element.567), channel_id=1, source_target_pairs={{1,0},{2,1},{3,2},{4,3},{5,4},{6,5},{7,6},{9,8},{10,9},{11,10},{12... | collective-permute-start | bytes 1179656 | tf_op jit(solution)/shard_map/ppermute | solution.py:20
  16.9 4.5 %copy-start.29 = (f32[4,256,127]{2,1,0:T(8,128)S(1)}, f32[4,256,127]{2,1,0:T(8,128)}, u32[]{:S(2)}) copy-start(f32[4,256,127]{2,1,0:T(8,128)} %get-tuple-element.573) | copy-start | bytes 1560580
  16.9 5.6 %copy-start.28 = (f32[4,256,127]{2,1,0:T(8,128)S(1)}, f32[4,256,127]{2,1,0:T(8,128)}, u32[]{:S(2)}) copy-start(f32[4,256,127]{2,1,0:T(8,128)} %get-tuple-element.574) | copy-start | bytes 1560580
  26.4 3.5 copy-start.32
  26.4 3.9 copy-start.33
  29.8 5.9 %copy-start.14 = (f32[4,256,128]{2,0,1:T(4,128)}, f32[4,256,128]{2,0,1:T(4,128)S(1)}, u32[]{:S(2)}) copy-start(f32[4,256,128]{2,0,1:T(4,128)S(1)} %get-tuple-element.553) | copy-start | bytes 1572868
  29.8 6.0 %copy-start.16 = (f32[4,256,128]{2,0,1:T(4,128)}, f32[4,256,128]{2,0,1:T(4,128)S(1)}, u32[]{:S(2)}) copy-start(f32[4,256,128]{2,0,1:T(4,128)S(1)} %get-tuple-element.552) | copy-start | bytes 1572868
  29.8 6.0 %copy-start.18 = (f32[4,256,128]{2,0,1:T(4,128)}, f32[4,256,128]{2,0,1:T(4,128)S(1)}, u32[]{:S(2)}) copy-start(f32[4,256,128]{2,0,1:T(4,128)S(1)} %get-tuple-element.551) | copy-start | bytes 1572868
  29.8 6.0 %copy-start.20 = (f32[4,256,128]{2,0,1:T(4,128)}, f32[4,256,128]{2,0,1:T(4,128)S(1)}, u32[]{:S(2)}) copy-start(f32[4,256,128]{2,0,1:T(4,128)S(1)} %get-tuple-element.550) | copy-start | bytes 1572868
  29.8 6.0 %copy-start.21 = (f32[4,256,128]{2,0,1:T(4,128)}, f32[4,256,128]{2,0,1:T(4,128)S(1)}, u32[]{:S(2)}) copy-start(f32[4,256,128]{2,0,1:T(4,128)S(1)} %get-tuple-element.547) | copy-start | bytes 1572868
  37.5 28.8 %all-to-all-start = ((f32[2,2,4,256,128]{4,2,0,1,3:T(4,128)}), f32[2,2,4,256,128]{4,2,0,1,3:T(4,128)S(1)}, u32[]{:S(2)}, u32[]{:S(2)}) async-start(f32[2,2,4,256,128]{4,2,0,1,3:T(4,128)} %stack.76), calls=%async_computation | async-start | bytes 4194304 | tf_op jit(solution)/shard_map/all_to_all | solution.py:112
  75.0 3.8 copy-start.34
  75.0 4.2 %copy-start.22 = (f32[4,256,128]{2,0,1:T(4,128)S(1)}, f32[4,256,128]{2,0,1:T(4,128)}, u32[]{:S(2)}) copy-start(f32[4,256,128]{2,0,1:T(4,128)} %copy-done.21) | copy-start | bytes 1572868
  75.0 29.9 %all-to-all-start.1 = ((f32[8,2,4,64,128]{4,3,2,1,0:T(8,128)}), f32[8,2,4,64,128]{4,3,2,1,0:T(8,128)S(1)}, u32[]{:S(2)}, u32[]{:S(2)}) async-start(f32[8,2,4,64,128]{4,3,2,1,0:T(8,128)} %copy.107), calls=%async_computation.1 | async-start | bytes 4194304 | tf_op jit(solution)/shard_map/all_to_all | solution.py:113
  79.3 3.7 copy-start.25
  80.4 3.4 copy-start.24
  108.5 8.4 %collective-permute-start = (f32[2,2,1,256,128]{4,3,2,1,0:T(8,128)}, f32[2,2,1,256,128]{4,3,2,1,0:T(8,128)}, u32[]{:S(2)}, u32[]{:S(2)}) collective-permute-start(f32[2,2,1,256,128]{4,3,2,1,0:T(8,128)} %get-tuple-element.694), channel_id=1, source_target_pairs={{1,0},{2,1},{3,2},{4,3},{5,4},{6,5},{7,6},{9,8},{10,9},{11,10},{12... | collective-permute-start | bytes 1572872 | tf_op jit(solution)/shard_map/while/body/eval_jaxpr/ppermute | solution.py:20
  109.7 7.1 %collective-permute-start.1 = (f32[2,2,1,256,128]{4,3,2,1,0:T(8,128)}, f32[2,2,1,256,128]{4,3,2,1,0:T(8,128)}, u32[]{:S(2)}, u32[]{:S(2)}) collective-permute-start(f32[2,2,1,256,128]{4,3,2,1,0:T(8,128)} %get-tuple-element.695), channel_id=1, source_target_pairs={{0,1},{1,2},{2,3},{3,4},{4,5},{5,6},{6,7},{8,9},{9,10},{10,11},{11... | collective-permute-start | bytes 1572872 | tf_op jit(solution)/shard_map/while/body/eval_jaxpr/ppermute | solution.py:17
  119.0 3.4 copy-start.4
  119.0 3.4 copy-start.5
  124.9 10.5 %collective-permute-start = (f32[2,2,1,256,128]{4,3,2,1,0:T(8,128)}, f32[2,2,1,256,128]{4,3,2,1,0:T(8,128)}, u32[]{:S(2)}, u32[]{:S(2)}) collective-permute-start(f32[2,2,1,256,128]{4,3,2,1,0:T(8,128)} %get-tuple-element.694), channel_id=1, source_target_pairs={{1,0},{2,1},{3,2},{4,3},{5,4},{6,5},{7,6},{9,8},{10,9},{11,10},{12... | collective-permute-start | bytes 1572872 | tf_op jit(solution)/shard_map/while/body/eval_jaxpr/ppermute | solution.py:20
  126.2 9.2 %collective-permute-start.1 = (f32[2,2,1,256,128]{4,3,2,1,0:T(8,128)}, f32[2,2,1,256,128]{4,3,2,1,0:T(8,128)}, u32[]{:S(2)}, u32[]{:S(2)}) collective-permute-start(f32[2,2,1,256,128]{4,3,2,1,0:T(8,128)} %get-tuple-element.695), channel_id=1, source_target_pairs={{0,1},{1,2},{2,3},{3,4},{4,5},{5,6},{6,7},{8,9},{9,10},{10,11},{11... | collective-permute-start | bytes 1572872 | tf_op jit(solution)/shard_map/while/body/eval_jaxpr/ppermute | solution.py:17
  137.6 3.4 copy-start.4
  137.6 3.4 copy-start.5
  143.5 10.7 %collective-permute-start = (f32[2,2,1,256,128]{4,3,2,1,0:T(8,128)}, f32[2,2,1,256,128]{4,3,2,1,0:T(8,128)}, u32[]{:S(2)}, u32[]{:S(2)}) collective-permute-start(f32[2,2,1,256,128]{4,3,2,1,0:T(8,128)} %get-tuple-element.694), channel_id=1, source_target_pairs={{1,0},{2,1},{3,2},{4,3},{5,4},{6,5},{7,6},{9,8},{10,9},{11,10},{12... | collective-permute-start | bytes 1572872 | tf_op jit(solution)/shard_map/while/body/eval_jaxpr/ppermute | solution.py:20
  144.8 9.4 %collective-permute-start.1 = (f32[2,2,1,256,128]{4,3,2,1,0:T(8,128)}, f32[2,2,1,256,128]{4,3,2,1,0:T(8,128)}, u32[]{:S(2)}, u32[]{:S(2)}) collective-permute-start(f32[2,2,1,256,128]{4,3,2,1,0:T(8,128)} %get-tuple-element.695), channel_id=1, source_target_pairs={{0,1},{1,2},{2,3},{3,4},{4,5},{5,6},{6,7},{8,9},{9,10},{10,11},{11... | collective-permute-start | bytes 1572872 | tf_op jit(solution)/shard_map/while/body/eval_jaxpr/ppermute | solution.py:17
  156.3 3.4 copy-start.4
  156.3 3.4 copy-start.5
  162.3 10.7 %collective-permute-start = (f32[2,2,1,256,128]{4,3,2,1,0:T(8,128)}, f32[2,2,1,256,128]{4,3,2,1,0:T(8,128)}, u32[]{:S(2)}, u32[]{:S(2)}) collective-permute-start(f32[2,2,1,256,128]{4,3,2,1,0:T(8,128)} %get-tuple-element.694), channel_id=1, source_target_pairs={{1,0},{2,1},{3,2},{4,3},{5,4},{6,5},{7,6},{9,8},{10,9},{11,10},{12... | collective-permute-start | bytes 1572872 | tf_op jit(solution)/shard_map/while/body/eval_jaxpr/ppermute | solution.py:20
  163.6 9.4 %collective-permute-start.1 = (f32[2,2,1,256,128]{4,3,2,1,0:T(8,128)}, f32[2,2,1,256,128]{4,3,2,1,0:T(8,128)}, u32[]{:S(2)}, u32[]{:S(2)}) collective-permute-start(f32[2,2,1,256,128]{4,3,2,1,0:T(8,128)} %get-tuple-element.695), channel_id=1, source_target_pairs={{0,1},{1,2},{2,3},{3,4},{4,5},{5,6},{6,7},{8,9},{9,10},{10,11},{11... | collective-permute-start | bytes 1572872 | tf_op jit(solution)/shard_map/while/body/eval_jaxpr/ppermute | solution.py:17
  175.1 3.4 copy-start.5
  181.0 10.7 %collective-permute-start = (f32[2,2,1,256,128]{4,3,2,1,0:T(8,128)}, f32[2,2,1,256,128]{4,3,2,1,0:T(8,128)}, u32[]{:S(2)}, u32[]{:S(2)}) collective-permute-start(f32[2,2,1,256,128]{4,3,2,1,0:T(8,128)} %get-tuple-element.694), channel_id=1, source_target_pairs={{1,0},{2,1},{3,2},{4,3},{5,4},{6,5},{7,6},{9,8},{10,9},{11,10},{12... | collective-permute-start | bytes 1572872 | tf_op jit(solution)/shard_map/while/body/eval_jaxpr/ppermute | solution.py:20
  182.3 9.4 %collective-permute-start.1 = (f32[2,2,1,256,128]{4,3,2,1,0:T(8,128)}, f32[2,2,1,256,128]{4,3,2,1,0:T(8,128)}, u32[]{:S(2)}, u32[]{:S(2)}) collective-permute-start(f32[2,2,1,256,128]{4,3,2,1,0:T(8,128)} %get-tuple-element.695), channel_id=1, source_target_pairs={{0,1},{1,2},{2,3},{3,4},{4,5},{5,6},{6,7},{8,9},{9,10},{10,11},{11... | collective-permute-start | bytes 1572872 | tf_op jit(solution)/shard_map/while/body/eval_jaxpr/ppermute | solution.py:17
  193.9 3.4 copy-start.4
  193.9 3.4 copy-start.5
  199.8 10.7 %collective-permute-start = (f32[2,2,1,256,128]{4,3,2,1,0:T(8,128)}, f32[2,2,1,256,128]{4,3,2,1,0:T(8,128)}, u32[]{:S(2)}, u32[]{:S(2)}) collective-permute-start(f32[2,2,1,256,128]{4,3,2,1,0:T(8,128)} %get-tuple-element.694), channel_id=1, source_target_pairs={{1,0},{2,1},{3,2},{4,3},{5,4},{6,5},{7,6},{9,8},{10,9},{11,10},{12... | collective-permute-start | bytes 1572872 | tf_op jit(solution)/shard_map/while/body/eval_jaxpr/ppermute | solution.py:20
  201.1 9.4 %collective-permute-start.1 = (f32[2,2,1,256,128]{4,3,2,1,0:T(8,128)}, f32[2,2,1,256,128]{4,3,2,1,0:T(8,128)}, u32[]{:S(2)}, u32[]{:S(2)}) collective-permute-start(f32[2,2,1,256,128]{4,3,2,1,0:T(8,128)} %get-tuple-element.695), channel_id=1, source_target_pairs={{0,1},{1,2},{2,3},{3,4},{4,5},{5,6},{6,7},{8,9},{9,10},{10,11},{11... | collective-permute-start | bytes 1572872 | tf_op jit(solution)/shard_map/while/body/eval_jaxpr/ppermute | solution.py:17
  212.6 3.4 copy-start.4
  212.6 3.4 copy-start.5
  218.6 10.7 %collective-permute-start = (f32[2,2,1,256,128]{4,3,2,1,0:T(8,128)}, f32[2,2,1,256,128]{4,3,2,1,0:T(8,128)}, u32[]{:S(2)}, u32[]{:S(2)}) collective-permute-start(f32[2,2,1,256,128]{4,3,2,1,0:T(8,128)} %get-tuple-element.694), channel_id=1, source_target_pairs={{1,0},{2,1},{3,2},{4,3},{5,4},{6,5},{7,6},{9,8},{10,9},{11,10},{12... | collective-permute-start | bytes 1572872 | tf_op jit(solution)/shard_map/while/body/eval_jaxpr/ppermute | solution.py:20
  219.9 9.4 %collective-permute-start.1 = (f32[2,2,1,256,128]{4,3,2,1,0:T(8,128)}, f32[2,2,1,256,128]{4,3,2,1,0:T(8,128)}, u32[]{:S(2)}, u32[]{:S(2)}) collective-permute-start(f32[2,2,1,256,128]{4,3,2,1,0:T(8,128)} %get-tuple-element.695), channel_id=1, source_target_pairs={{0,1},{1,2},{2,3},{3,4},{4,5},{5,6},{6,7},{8,9},{9,10},{10,11},{11... | collective-permute-start | bytes 1572872 | tf_op jit(solution)/shard_map/while/body/eval_jaxpr/ppermute | solution.py:17
  231.4 3.4 copy-start.5
  237.3 10.7 %collective-permute-start = (f32[2,2,1,256,128]{4,3,2,1,0:T(8,128)}, f32[2,2,1,256,128]{4,3,2,1,0:T(8,128)}, u32[]{:S(2)}, u32[]{:S(2)}) collective-permute-start(f32[2,2,1,256,128]{4,3,2,1,0:T(8,128)} %get-tuple-element.694), channel_id=1, source_target_pairs={{1,0},{2,1},{3,2},{4,3},{5,4},{6,5},{7,6},{9,8},{10,9},{11,10},{12... | collective-permute-start | bytes 1572872 | tf_op jit(solution)/shard_map/while/body/eval_jaxpr/ppermute | solution.py:20
  238.6 9.4 %collective-permute-start.1 = (f32[2,2,1,256,128]{4,3,2,1,0:T(8,128)}, f32[2,2,1,256,128]{4,3,2,1,0:T(8,128)}, u32[]{:S(2)}, u32[]{:S(2)}) collective-permute-start(f32[2,2,1,256,128]{4,3,2,1,0:T(8,128)} %get-tuple-element.695), channel_id=1, source_target_pairs={{0,1},{1,2},{2,3},{3,4},{4,5},{5,6},{6,7},{8,9},{9,10},{10,11},{11... | collective-permute-start | bytes 1572872 | tf_op jit(solution)/shard_map/while/body/eval_jaxpr/ppermute | solution.py:17
  250.1 3.4 copy-start.5
  256.1 10.7 %collective-permute-start = (f32[2,2,1,256,128]{4,3,2,1,0:T(8,128)}, f32[2,2,1,256,128]{4,3,2,1,0:T(8,128)}, u32[]{:S(2)}, u32[]{:S(2)}) collective-permute-start(f32[2,2,1,256,128]{4,3,2,1,0:T(8,128)} %get-tuple-element.694), channel_id=1, source_target_pairs={{1,0},{2,1},{3,2},{4,3},{5,4},{6,5},{7,6},{9,8},{10,9},{11,10},{12... | collective-permute-start | bytes 1572872 | tf_op jit(solution)/shard_map/while/body/eval_jaxpr/ppermute | solution.py:20
  257.4 9.4 %collective-permute-start.1 = (f32[2,2,1,256,128]{4,3,2,1,0:T(8,128)}, f32[2,2,1,256,128]{4,3,2,1,0:T(8,128)}, u32[]{:S(2)}, u32[]{:S(2)}) collective-permute-start(f32[2,2,1,256,128]{4,3,2,1,0:T(8,128)} %get-tuple-element.695), channel_id=1, source_target_pairs={{0,1},{1,2},{2,3},{3,4},{4,5},{5,6},{6,7},{8,9},{9,10},{10,11},{11... | collective-permute-start | bytes 1572872 | tf_op jit(solution)/shard_map/while/body/eval_jaxpr/ppermute | solution.py:17
  268.9 3.4 copy-start.5
  274.9 10.7 %collective-permute-start = (f32[2,2,1,256,128]{4,3,2,1,0:T(8,128)}, f32[2,2,1,256,128]{4,3,2,1,0:T(8,128)}, u32[]{:S(2)}, u32[]{:S(2)}) collective-permute-start(f32[2,2,1,256,128]{4,3,2,1,0:T(8,128)} %get-tuple-element.694), channel_id=1, source_target_pairs={{1,0},{2,1},{3,2},{4,3},{5,4},{6,5},{7,6},{9,8},{10,9},{11,10},{12... | collective-permute-start | bytes 1572872 | tf_op jit(solution)/shard_map/while/body/eval_jaxpr/ppermute | solution.py:20
  276.1 9.4 %collective-permute-start.1 = (f32[2,2,1,256,128]{4,3,2,1,0:T(8,128)}, f32[2,2,1,256,128]{4,3,2,1,0:T(8,128)}, u32[]{:S(2)}, u32[]{:S(2)}) collective-permute-start(f32[2,2,1,256,128]{4,3,2,1,0:T(8,128)} %get-tuple-element.695), channel_id=1, source_target_pairs={{0,1},{1,2},{2,3},{3,4},{4,5},{5,6},{6,7},{8,9},{9,10},{10,11},{11... | collective-permute-start | bytes 1572872 | tf_op jit(solution)/shard_map/while/body/eval_jaxpr/ppermute | solution.py:17
  287.7 3.4 copy-start.5
  293.6 10.7 %collective-permute-start = (f32[2,2,1,256,128]{4,3,2,1,0:T(8,128)}, f32[2,2,1,256,128]{4,3,2,1,0:T(8,128)}, u32[]{:S(2)}, u32[]{:S(2)}) collective-permute-start(f32[2,2,1,256,128]{4,3,2,1,0:T(8,128)} %get-tuple-element.694), channel_id=1, source_target_pairs={{1,0},{2,1},{3,2},{4,3},{5,4},{6,5},{7,6},{9,8},{10,9},{11,10},{12... | collective-permute-start | bytes 1572872 | tf_op jit(solution)/shard_map/while/body/eval_jaxpr/ppermute | solution.py:20
  294.9 9.4 %collective-permute-start.1 = (f32[2,2,1,256,128]{4,3,2,1,0:T(8,128)}, f32[2,2,1,256,128]{4,3,2,1,0:T(8,128)}, u32[]{:S(2)}, u32[]{:S(2)}) collective-permute-start(f32[2,2,1,256,128]{4,3,2,1,0:T(8,128)} %get-tuple-element.695), channel_id=1, source_target_pairs={{0,1},{1,2},{2,3},{3,4},{4,5},{5,6},{6,7},{8,9},{9,10},{10,11},{11... | collective-permute-start | bytes 1572872 | tf_op jit(solution)/shard_map/while/body/eval_jaxpr/ppermute | solution.py:17
  306.4 3.4 copy-start.5
  312.4 10.7 %collective-permute-start = (f32[2,2,1,256,128]{4,3,2,1,0:T(8,128)}, f32[2,2,1,256,128]{4,3,2,1,0:T(8,128)}, u32[]{:S(2)}, u32[]{:S(2)}) collective-permute-start(f32[2,2,1,256,128]{4,3,2,1,0:T(8,128)} %get-tuple-element.694), channel_id=1, source_target_pairs={{1,0},{2,1},{3,2},{4,3},{5,4},{6,5},{7,6},{9,8},{10,9},{11,10},{12... | collective-permute-start | bytes 1572872 | tf_op jit(solution)/shard_map/while/body/eval_jaxpr/ppermute | solution.py:20
  313.7 9.4 %collective-permute-start.1 = (f32[2,2,1,256,128]{4,3,2,1,0:T(8,128)}, f32[2,2,1,256,128]{4,3,2,1,0:T(8,128)}, u32[]{:S(2)}, u32[]{:S(2)}) collective-permute-start(f32[2,2,1,256,128]{4,3,2,1,0:T(8,128)} %get-tuple-element.695), channel_id=1, source_target_pairs={{0,1},{1,2},{2,3},{3,4},{4,5},{5,6},{6,7},{8,9},{9,10},{10,11},{11... | collective-permute-start | bytes 1572872 | tf_op jit(solution)/shard_map/while/body/eval_jaxpr/ppermute | solution.py:17
  325.2 3.4 copy-start.5
  332.8 28.8 %all-to-all-start.2 = ((f32[2,2,4,256,128]{4,2,1,0,3:T(4,128)}), f32[2,2,4,256,128]{4,2,1,0,3:T(4,128)S(1)}, u32[]{:S(2)}, u32[]{:S(2)}) async-start(f32[2,2,4,256,128]{4,2,1,0,3:T(4,128)} %copy.118), calls=%async_computation.2 | async-start | bytes 4194304 | tf_op jit(solution)/shard_map/all_to_all | solution.py:161
  370.3 29.8 %all-to-all-start.3 = ((f32[8,2,4,64,128]{4,3,2,1,0:T(8,128)}), f32[8,2,4,64,128]{4,3,2,1,0:T(8,128)S(1)}, u32[]{:S(2)}, u32[]{:S(2)}) async-start(f32[8,2,4,64,128]{4,3,2,1,0:T(8,128)} %copy.121), calls=%async_computation.3 | async-start | bytes 4194304 | tf_op jit(solution)/shard_map/all_to_all | solution.py:162
  (101 other events, 244.5 us)
where the time goes:
time: 404 us; the launch traced here: 402 us
  local copies, waits for them, and re-layouts  115 us (28%)
  starting transfers between devices  110 us (27%)
  waiting for transfers between devices  95.7 us (24%)
  other arithmetic  72.4 us (18%)
  matrix products  6.04 us (1%)
    ppermute x13, starting transfers between devices, padded_2(): lax.ppermute(lax.slice_in_dim(block, block.shape[dim] - width, None, axis...  72.5 us
    sub x12, other arithmetic, operate(): return diag_sum * core - total  40.2 us
    slice x26, local copies, waits for them, and re-layouts, along(): lax.slice_in_dim(core, 0, length - 1, axis=axis)  38.9 us
    all_to_all x1, waiting for transfers between devices, shards(): back = lax.all_to_all(back, 'tm', split_axis=0, concat_axis=3, tiled=True)  26.1 us
    while x216, local copies, waits for them, and re-layouts  25.5 us
    all_to_all x1, waiting for transfers between devices, shards(): lax.all_to_all(solution, 'tm', split_axis=3, concat_axis=0, tiled=True)  24.7 us
    all_to_all x1, waiting for transfers between devices, shards(): lax.all_to_all(field, 'tm', split_axis=3, concat_axis=0, tiled=True)  24.5 us
    all_to_all x1, waiting for transfers between devices, shards(): lax.all_to_all(spectral, 'tm', split_axis=0, concat_axis=3, tiled=True)  20.2 us
  transfers between devices with their start and end apart: 31, of which 4 were waited for; matrix products, arithmetic and copies ran while one was open for 15% of the time, Pallas kernels for 0%

commit v1 on v0

--- a/solution.py
+++ b/solution.py
@@ -110,7 +110,12 @@
     field = jnp.stack([weighted, jnp.zeros_like(weighted)], 1)
     local_index = device * local_steps + lax.iota(jnp.int32, local_steps)
     spectral = forward_time(lax.all_to_all(field, "tm", split_axis=3, concat_axis=0, tiled=True))
-    spectral = lax.all_to_all(spectral, "tm", split_axis=0, concat_axis=3, tiled=True)
+    spectral = jnp.concatenate(
+        lax.all_to_all(
+            jnp.stack(jnp.split(spectral, lax.axis_size("tm"), axis=0), axis=0), "tm", 0, 0
+        ),
+        axis=3,
+    )
     chooser = (local_index[:, None] == lax.iota(jnp.int32, total_steps)[None, :]).astype(
         jnp.float32
     )

time: 404 us -> 403 us (level)
    unnamed x68 -> x72, local copies, waits for them, and re-layouts: 17.9 us -> 17.9 us
where the time goes in v1:
time: 403 us; the launch traced here: 401 us
  local copies, waits for them, and re-layouts  113 us (28%)
  starting transfers between devices  110 us (27%)
  waiting for transfers between devices  95.7 us (24%)
  other arithmetic  73.8 us (18%)
  matrix products  5.1 us (1%)
    ppermute x13, starting transfers between devices, padded_2(): lax.ppermute(lax.slice_in_dim(block, block.shape[dim] - width, None, axis...  72.5 us
    sub x12, other arithmetic, operate(): return diag_sum * core - total  40.2 us
    slice x26, local copies, waits for them, and re-layouts, along(): lax.slice_in_dim(core, 0, length - 1, axis=axis)  38.8 us
    all_to_all x1, waiting for transfers between devices, shards(): back = lax.all_to_all(back, 'tm', split_axis=0, concat_axis=3, tiled=True)  26.1 us
    while x216, local copies, waits for them, and re-layouts  25.5 us
    all_to_all x1, waiting for transfers between devices, shards(): lax.all_to_all(solution, 'tm', split_axis=3, concat_axis=0, tiled=True)  24.7 us
    all_to_all x1, waiting for transfers between devices, shards(): lax.all_to_all(field, 'tm', split_axis=3, concat_axis=0, tiled=True)  24.6 us
    all_to_all x1, waiting for transfers between devices, shards(): lax.all_to_all(jnp.stack(jnp.split(spectral, lax.axis_size('tm'), axis=0)...  20.2 us
  transfers between devices with their start and end apart: 31, of which 4 were waited for; matrix products, arithmetic and copies ran while one was open for 15% of the time, Pallas kernels for 0%

profile of v1, /device:TPU:0, one launch (start us, length us, event | category | flops | bytes accessed | tf_op | source)
XLA Modules:
  0.0 401.4 jit_solution(11748597203675588995)
XLA Ops:
  2.4 5.7 %collective-permute-start.2 = (f32[4,256,128]{2,0,1:T(4,128)}, f32[4,256,128]{2,0,1:T(4,128)}, u32[]{:S(2)}, u32[]{:S(2)}) collective-permute-start(f32[4,256,128]{2,0,1:T(4,128)} %bitcast.144), channel_id=1, source_target_pairs={{0,8},{8,16},{16,24},{1,9},{9,17},{17,25},{2,10},{10,18},{18,26},{... | collective-permute-start | bytes 1572872 | tf_op jit(solution)/shard_map/ppermute | solution.py:28
  9.1 1.5 pad_maximum_fusion.12
  16.8 2.3 copy.99
  19.0 2.2 copy.100
  24.3 2.0 multiply_bitcast_fusion.1
  26.3 3.4 add_add_fusion
  30.2 1.6 copy-done.23
  31.8 3.9 fusion.37
  35.7 1.7 stack.91
  37.4 3.8 all-to-all-start
  41.6 24.6 %all-to-all-done = f32[2,2,4,256,128]{4,2,0,1,3:T(4,128)S(1)} async-done(((f32[2,2,4,256,128]{4,2,0,1,3:T(4,128)}), f32[2,2,4,256,128]{4,2,0,1,3:T(4,128)S(1)}, u32[]{:S(2)}, u32[]{:S(2)}) %all-to-all-start) | async-done | bytes 2097184 | tf_op jit(solution)/shard_map/all_to_all | solution.py:112
  66.2 2.0 copy.108
  68.2 1.7 reshape.231
  69.9 1.9 fusion.83
  72.3 1.5 pad_maximum_fusion.3
  73.8 3.7 all-to-all-start.1
  83.5 20.2 %all-to-all-done.1 = f32[4,2,2,4,64,128]{5,4,3,2,1,0:T(8,128)S(1)} async-done(((f32[4,2,2,4,64,128]{5,4,3,2,1,0:T(8,128)}), f32[4,2,2,4,64,128]{5,4,3,2,1,0:T(8,128)S(1)}, u32[]{:S(2)}, u32[]{:S(2)}) %all-to-all-start.1) | async-done | bytes 2097184 | tf_op jit(solution)/shard_map/all_to_all | solution.py:114
  103.9 1.9 multiply_subtract_fusion
  106.1 222.9 %while.17 = (s32[]{:T(128)}, f32[2,2,4,256,128]{4,3,2,1,0:T(8,128)S(1)}, f32[2,4,256,128]{3,2,1,0:T(8,128)}, f32[2,1,1,1]{0,3,2,1:T(1,128)S(1)}, f32[2,1,1,1]{0,...) while((s32[]{:T(128)}, ...), condition=%wide.region_1.2_spmd.clone.clone, body=%wide.region_0.1_spmd.clone.clone.sunk | while | flops 16252937 | bytes 94683824 | solution.py:165
  108.5 3.8 collective-permute-start.1
  112.4 2.4 fusion.94
  117.8 3.3 fusion.95
  125.0 5.9 %collective-permute-start.1 = (f32[2,2,1,256,128]{4,3,2,1,0:T(8,128)}, f32[2,2,1,256,128]{4,3,2,1,0:T(8,128)}, u32[]{:S(2)}, u32[]{:S(2)}) collective-permute-start(f32[2,2,1,256,128]{4,3,2,1,0:T(8,128)} %get-tuple-element.683), channel_id=1, source_target_pairs={{0,1},{1,2},{2,3},{3,4},{4,5},{5,6},{6,7},{8,9},{9,10},{10,11},{11... | collective-permute-start | bytes 1572872 | tf_op jit(solution)/shard_map/while/body/eval_jaxpr/ppermute | solution.py:17
  131.0 2.4 fusion.94
  136.4 3.3 fusion.95
  143.6 6.1 %collective-permute-start.1 = (f32[2,2,1,256,128]{4,3,2,1,0:T(8,128)}, f32[2,2,1,256,128]{4,3,2,1,0:T(8,128)}, u32[]{:S(2)}, u32[]{:S(2)}) collective-permute-start(f32[2,2,1,256,128]{4,3,2,1,0:T(8,128)} %get-tuple-element.683), channel_id=1, source_target_pairs={{0,1},{1,2},{2,3},{3,4},{4,5},{5,6},{6,7},{8,9},{9,10},{10,11},{11... | collective-permute-start | bytes 1572872 | tf_op jit(solution)/shard_map/while/body/eval_jaxpr/ppermute | solution.py:17
  149.8 2.4 fusion.94
  155.2 3.3 fusion.95
  162.4 6.1 %collective-permute-start.1 = (f32[2,2,1,256,128]{4,3,2,1,0:T(8,128)}, f32[2,2,1,256,128]{4,3,2,1,0:T(8,128)}, u32[]{:S(2)}, u32[]{:S(2)}) collective-permute-start(f32[2,2,1,256,128]{4,3,2,1,0:T(8,128)} %get-tuple-element.683), channel_id=1, source_target_pairs={{0,1},{1,2},{2,3},{3,4},{4,5},{5,6},{6,7},{8,9},{9,10},{10,11},{11... | collective-permute-start | bytes 1572872 | tf_op jit(solution)/shard_map/while/body/eval_jaxpr/ppermute | solution.py:17
  168.5 2.4 fusion.94
  173.9 3.3 fusion.95
  181.2 6.1 %collective-permute-start.1 = (f32[2,2,1,256,128]{4,3,2,1,0:T(8,128)}, f32[2,2,1,256,128]{4,3,2,1,0:T(8,128)}, u32[]{:S(2)}, u32[]{:S(2)}) collective-permute-start(f32[2,2,1,256,128]{4,3,2,1,0:T(8,128)} %get-tuple-element.683), channel_id=1, source_target_pairs={{0,1},{1,2},{2,3},{3,4},{4,5},{5,6},{6,7},{8,9},{9,10},{10,11},{11... | collective-permute-start | bytes 1572872 | tf_op jit(solution)/shard_map/while/body/eval_jaxpr/ppermute | solution.py:17
  187.3 2.4 fusion.94
  192.7 3.3 fusion.95
  200.0 6.1 %collective-permute-start.1 = (f32[2,2,1,256,128]{4,3,2,1,0:T(8,128)}, f32[2,2,1,256,128]{4,3,2,1,0:T(8,128)}, u32[]{:S(2)}, u32[]{:S(2)}) collective-permute-start(f32[2,2,1,256,128]{4,3,2,1,0:T(8,128)} %get-tuple-element.683), channel_id=1, source_target_pairs={{0,1},{1,2},{2,3},{3,4},{4,5},{5,6},{6,7},{8,9},{9,10},{10,11},{11... | collective-permute-start | bytes 1572872 | tf_op jit(solution)/shard_map/while/body/eval_jaxpr/ppermute | solution.py:17
  206.1 2.4 fusion.94
  211.5 3.3 fusion.95
  218.7 6.1 %collective-permute-start.1 = (f32[2,2,1,256,128]{4,3,2,1,0:T(8,128)}, f32[2,2,1,256,128]{4,3,2,1,0:T(8,128)}, u32[]{:S(2)}, u32[]{:S(2)}) collective-permute-start(f32[2,2,1,256,128]{4,3,2,1,0:T(8,128)} %get-tuple-element.683), channel_id=1, source_target_pairs={{0,1},{1,2},{2,3},{3,4},{4,5},{5,6},{6,7},{8,9},{9,10},{10,11},{11... | collective-permute-start | bytes 1572872 | tf_op jit(solution)/shard_map/while/body/eval_jaxpr/ppermute | solution.py:17
  224.9 2.4 fusion.94
  230.3 3.3 fusion.95
  237.5 6.1 %collective-permute-start.1 = (f32[2,2,1,256,128]{4,3,2,1,0:T(8,128)}, f32[2,2,1,256,128]{4,3,2,1,0:T(8,128)}, u32[]{:S(2)}, u32[]{:S(2)}) collective-permute-start(f32[2,2,1,256,128]{4,3,2,1,0:T(8,128)} %get-tuple-element.683), channel_id=1, source_target_pairs={{0,1},{1,2},{2,3},{3,4},{4,5},{5,6},{6,7},{8,9},{9,10},{10,11},{11... | collective-permute-start | bytes 1572872 | tf_op jit(solution)/shard_map/while/body/eval_jaxpr/ppermute | solution.py:17
  243.7 2.4 fusion.94
  249.1 3.3 fusion.95
  256.3 6.1 %collective-permute-start.1 = (f32[2,2,1,256,128]{4,3,2,1,0:T(8,128)}, f32[2,2,1,256,128]{4,3,2,1,0:T(8,128)}, u32[]{:S(2)}, u32[]{:S(2)}) collective-permute-start(f32[2,2,1,256,128]{4,3,2,1,0:T(8,128)} %get-tuple-element.683), channel_id=1, source_target_pairs={{0,1},{1,2},{2,3},{3,4},{4,5},{5,6},{6,7},{8,9},{9,10},{10,11},{11... | collective-permute-start | bytes 1572872 | tf_op jit(solution)/shard_map/while/body/eval_jaxpr/ppermute | solution.py:17
  262.4 2.4 fusion.94
  267.8 3.3 fusion.95
  275.1 6.1 %collective-permute-start.1 = (f32[2,2,1,256,128]{4,3,2,1,0:T(8,128)}, f32[2,2,1,256,128]{4,3,2,1,0:T(8,128)}, u32[]{:S(2)}, u32[]{:S(2)}) collective-permute-start(f32[2,2,1,256,128]{4,3,2,1,0:T(8,128)} %get-tuple-element.683), channel_id=1, source_target_pairs={{0,1},{1,2},{2,3},{3,4},{4,5},{5,6},{6,7},{8,9},{9,10},{10,11},{11... | collective-permute-start | bytes 1572872 | tf_op jit(solution)/shard_map/while/body/eval_jaxpr/ppermute | solution.py:17
  281.2 2.4 fusion.94
  286.6 3.3 fusion.95
  293.9 6.1 %collective-permute-start.1 = (f32[2,2,1,256,128]{4,3,2,1,0:T(8,128)}, f32[2,2,1,256,128]{4,3,2,1,0:T(8,128)}, u32[]{:S(2)}, u32[]{:S(2)}) collective-permute-start(f32[2,2,1,256,128]{4,3,2,1,0:T(8,128)} %get-tuple-element.683), channel_id=1, source_target_pairs={{0,1},{1,2},{2,3},{3,4},{4,5},{5,6},{6,7},{8,9},{9,10},{10,11},{11... | collective-permute-start | bytes 1572872 | tf_op jit(solution)/shard_map/while/body/eval_jaxpr/ppermute | solution.py:17
  300.0 2.4 fusion.94
  305.4 3.3 fusion.95
  312.6 6.1 %collective-permute-start.1 = (f32[2,2,1,256,128]{4,3,2,1,0:T(8,128)}, f32[2,2,1,256,128]{4,3,2,1,0:T(8,128)}, u32[]{:S(2)}, u32[]{:S(2)}) collective-permute-start(f32[2,2,1,256,128]{4,3,2,1,0:T(8,128)} %get-tuple-element.683), channel_id=1, source_target_pairs={{0,1},{1,2},{2,3},{3,4},{4,5},{5,6},{6,7},{8,9},{9,10},{10,11},{11... | collective-permute-start | bytes 1572872 | tf_op jit(solution)/shard_map/while/body/eval_jaxpr/ppermute | solution.py:17
  318.8 2.4 fusion.94
  324.2 3.3 fusion.95
  329.0 2.7 copy.66
  331.7 3.8 all-to-all-start.2
  335.9 24.7 %all-to-all-done.2 = f32[2,2,4,256,128]{4,2,1,0,3:T(4,128)S(1)} async-done(((f32[2,2,4,256,128]{4,2,1,0,3:T(4,128)}), f32[2,2,4,256,128]{4,2,1,0,3:T(4,128)S(1)}, u32[]{:S(2)}, u32[]{:S(2)}) %all-to-all-start.2) | async-done | bytes 2097184 | tf_op jit(solution)/shard_map/all_to_all | solution.py:166
  360.6 2.0 copy.107
  362.5 1.7 reshape.236
  364.7 2.8 fusion.28
  367.5 1.7 copy.69
  369.3 3.6 all-to-all-start.3
  372.9 26.1 %all-to-all-done.3 = f32[8,2,4,64,128]{4,3,2,1,0:T(8,128)S(1)} async-done(((f32[8,2,4,64,128]{4,3,2,1,0:T(8,128)}), f32[8,2,4,64,128]{4,3,2,1,0:T(8,128)S(1)}, u32[]{:S(2)}, u32[]{:S(2)}) %all-to-all-start.3) | async-done | bytes 2097184 | tf_op jit(solution)/shard_map/all_to_all | solution.py:167
  (412 shorter events, 103.6 us)
Async XLA Ops:
  0.0 77.8 %copy-start = (f32[8]{0:T(128)S(1)}, f32[8]{0:T(128)}, u32[]{:S(2)}) copy-start(f32[8]{0:T(128)} %param.13) | copy-start | bytes 100
  0.0 8.0 %copy-start.12 = (f32[2,4,256,128]{3,2,1,0:T(8,128)S(1)}, f32[2,4,256,128]{3,2,1,0:T(8,128)}, u32[]{:S(2)}) copy-start(f32[2,4,256,128]{3,2,1,0:T(8,128)} %param.8) | copy-start | bytes 3145732
  0.0 8.7 %copy-start.6 = (f32[4,256,128]{2,1,0:T(8,128)S(1)}, f32[4,256,128]{2,1,0:T(8,128)}, u32[]{:S(2)}) copy-start(f32[4,256,128]{2,1,0:T(8,128)} %param.10) | copy-start | bytes 1572868
  2.4 27.4 %collective-permute-start.2 = (f32[4,256,128]{2,0,1:T(4,128)}, f32[4,256,128]{2,0,1:T(4,128)}, u32[]{:S(2)}, u32[]{:S(2)}) collective-permute-start(f32[4,256,128]{2,0,1:T(4,128)} %bitcast.144), channel_id=1, source_target_pairs={{0,8},{8,16},{16,24},{1,9},{9,17},{17,25},{2,10},{10,18},{18,26},{... | collective-permute-start | bytes 1572872 | tf_op jit(solution)/shard_map/ppermute | solution.py:28
  10.6 13.7 %collective-permute-start.3 = (f32[3,1,256,128]{3,1,0,2:T(1,128)}, f32[3,1,256,128]{3,1,0,2:T(1,128)S(1)}, u32[]{:S(2)}, u32[]{:S(2)}) collective-permute-start(f32[3,1,256,128]{3,1,0,2:T(1,128)} %get-tuple-element.554), channel_id=1, source_target_pairs={{0,1},{1,2},{2,3},{3,4},{4,5},{5,6},{6,7},{8,9},{9,10},{10,11},{11... | collective-permute-start | bytes 1179656 | tf_op jit(solution)/shard_map/ppermute | solution.py:17
  12.1 12.2 %collective-permute-start.4 = (f32[3,1,256,128]{3,1,0,2:T(1,128)}, f32[3,1,256,128]{3,1,0,2:T(1,128)}, u32[]{:S(2)}, u32[]{:S(2)}) collective-permute-start(f32[3,1,256,128]{3,1,0,2:T(1,128)} %get-tuple-element.555), channel_id=1, source_target_pairs={{1,0},{2,1},{3,2},{4,3},{5,4},{6,5},{7,6},{9,8},{10,9},{11,10},{12... | collective-permute-start | bytes 1179656 | tf_op jit(solution)/shard_map/ppermute | solution.py:20
  16.8 4.4 %copy-start.29 = (f32[4,256,127]{2,1,0:T(8,128)S(1)}, f32[4,256,127]{2,1,0:T(8,128)}, u32[]{:S(2)}) copy-start(f32[4,256,127]{2,1,0:T(8,128)} %get-tuple-element.561) | copy-start | bytes 1560580
  16.8 5.6 %copy-start.28 = (f32[4,256,127]{2,1,0:T(8,128)S(1)}, f32[4,256,127]{2,1,0:T(8,128)}, u32[]{:S(2)}) copy-start(f32[4,256,127]{2,1,0:T(8,128)} %get-tuple-element.562) | copy-start | bytes 1560580
  26.3 3.5 copy-start.32
  26.3 3.9 copy-start.33
  29.7 5.9 %copy-start.14 = (f32[4,256,128]{2,0,1:T(4,128)}, f32[4,256,128]{2,0,1:T(4,128)S(1)}, u32[]{:S(2)}) copy-start(f32[4,256,128]{2,0,1:T(4,128)S(1)} %get-tuple-element.537) | copy-start | bytes 1572868
  29.7 6.0 %copy-start.16 = (f32[4,256,128]{2,0,1:T(4,128)}, f32[4,256,128]{2,0,1:T(4,128)S(1)}, u32[]{:S(2)}) copy-start(f32[4,256,128]{2,0,1:T(4,128)S(1)} %get-tuple-element.536) | copy-start | bytes 1572868
  29.7 6.0 %copy-start.18 = (f32[4,256,128]{2,0,1:T(4,128)}, f32[4,256,128]{2,0,1:T(4,128)S(1)}, u32[]{:S(2)}) copy-start(f32[4,256,128]{2,0,1:T(4,128)S(1)} %get-tuple-element.535) | copy-start | bytes 1572868
  29.7 6.0 %copy-start.20 = (f32[4,256,128]{2,0,1:T(4,128)}, f32[4,256,128]{2,0,1:T(4,128)S(1)}, u32[]{:S(2)}) copy-start(f32[4,256,128]{2,0,1:T(4,128)S(1)} %get-tuple-element.534) | copy-start | bytes 1572868
  29.7 6.0 %copy-start.21 = (f32[4,256,128]{2,0,1:T(4,128)}, f32[4,256,128]{2,0,1:T(4,128)S(1)}, u32[]{:S(2)}) copy-start(f32[4,256,128]{2,0,1:T(4,128)S(1)} %get-tuple-element.531) | copy-start | bytes 1572868
  37.4 28.8 %all-to-all-start = ((f32[2,2,4,256,128]{4,2,0,1,3:T(4,128)}), f32[2,2,4,256,128]{4,2,0,1,3:T(4,128)S(1)}, u32[]{:S(2)}, u32[]{:S(2)}) async-start(f32[2,2,4,256,128]{4,2,0,1,3:T(4,128)} %stack.91), calls=%async_computation | async-start | bytes 4194304 | tf_op jit(solution)/shard_map/all_to_all | solution.py:112
  73.8 3.8 copy-start.34
  73.8 4.2 %copy-start.22 = (f32[4,256,128]{2,0,1:T(4,128)S(1)}, f32[4,256,128]{2,0,1:T(4,128)}, u32[]{:S(2)}) copy-start(f32[4,256,128]{2,0,1:T(4,128)} %copy-done.21) | copy-start | bytes 1572868
  73.8 29.9 %all-to-all-start.1 = ((f32[4,2,2,4,64,128]{5,4,3,2,1,0:T(8,128)}), f32[4,2,2,4,64,128]{5,4,3,2,1,0:T(8,128)S(1)}, u32[]{:S(2)}, u32[]{:S(2)}) async-start(f32[4,2,2,4,64,128]{5,4,3,2,1,0:T(8,128)} %pad_maximum_fusion.3), calls=%async_computation.1 | async-start | bytes 4194304 | tf_op jit(solution)/shard_map/all_to_all | solution.py:114
  78.0 3.7 copy-start.25
  79.2 3.4 copy-start.24
  107.3 8.4 %collective-permute-start = (f32[2,2,1,256,128]{4,3,2,1,0:T(8,128)}, f32[2,2,1,256,128]{4,3,2,1,0:T(8,128)}, u32[]{:S(2)}, u32[]{:S(2)}) collective-permute-start(f32[2,2,1,256,128]{4,3,2,1,0:T(8,128)} %get-tuple-element.682), channel_id=1, source_target_pairs={{1,0},{2,1},{3,2},{4,3},{5,4},{6,5},{7,6},{9,8},{10,9},{11,10},{12... | collective-permute-start | bytes 1572872 | tf_op jit(solution)/shard_map/while/body/eval_jaxpr/ppermute | solution.py:20
  108.5 7.1 %collective-permute-start.1 = (f32[2,2,1,256,128]{4,3,2,1,0:T(8,128)}, f32[2,2,1,256,128]{4,3,2,1,0:T(8,128)}, u32[]{:S(2)}, u32[]{:S(2)}) collective-permute-start(f32[2,2,1,256,128]{4,3,2,1,0:T(8,128)} %get-tuple-element.683), channel_id=1, source_target_pairs={{0,1},{1,2},{2,3},{3,4},{4,5},{5,6},{6,7},{8,9},{9,10},{10,11},{11... | collective-permute-start | bytes 1572872 | tf_op jit(solution)/shard_map/while/body/eval_jaxpr/ppermute | solution.py:17
  117.8 3.4 copy-start.4
  117.8 3.4 copy-start.5
  123.7 10.5 %collective-permute-start = (f32[2,2,1,256,128]{4,3,2,1,0:T(8,128)}, f32[2,2,1,256,128]{4,3,2,1,0:T(8,128)}, u32[]{:S(2)}, u32[]{:S(2)}) collective-permute-start(f32[2,2,1,256,128]{4,3,2,1,0:T(8,128)} %get-tuple-element.682), channel_id=1, source_target_pairs={{1,0},{2,1},{3,2},{4,3},{5,4},{6,5},{7,6},{9,8},{10,9},{11,10},{12... | collective-permute-start | bytes 1572872 | tf_op jit(solution)/shard_map/while/body/eval_jaxpr/ppermute | solution.py:20
  125.0 9.2 %collective-permute-start.1 = (f32[2,2,1,256,128]{4,3,2,1,0:T(8,128)}, f32[2,2,1,256,128]{4,3,2,1,0:T(8,128)}, u32[]{:S(2)}, u32[]{:S(2)}) collective-permute-start(f32[2,2,1,256,128]{4,3,2,1,0:T(8,128)} %get-tuple-element.683), channel_id=1, source_target_pairs={{0,1},{1,2},{2,3},{3,4},{4,5},{5,6},{6,7},{8,9},{9,10},{10,11},{11... | collective-permute-start | bytes 1572872 | tf_op jit(solution)/shard_map/while/body/eval_jaxpr/ppermute | solution.py:17
  136.4 3.4 copy-start.4
  136.4 3.4 copy-start.5
  142.3 10.7 %collective-permute-start = (f32[2,2,1,256,128]{4,3,2,1,0:T(8,128)}, f32[2,2,1,256,128]{4,3,2,1,0:T(8,128)}, u32[]{:S(2)}, u32[]{:S(2)}) collective-permute-start(f32[2,2,1,256,128]{4,3,2,1,0:T(8,128)} %get-tuple-element.682), channel_id=1, source_target_pairs={{1,0},{2,1},{3,2},{4,3},{5,4},{6,5},{7,6},{9,8},{10,9},{11,10},{12... | collective-permute-start | bytes 1572872 | tf_op jit(solution)/shard_map/while/body/eval_jaxpr/ppermute | solution.py:20
  143.6 9.4 %collective-permute-start.1 = (f32[2,2,1,256,128]{4,3,2,1,0:T(8,128)}, f32[2,2,1,256,128]{4,3,2,1,0:T(8,128)}, u32[]{:S(2)}, u32[]{:S(2)}) collective-permute-start(f32[2,2,1,256,128]{4,3,2,1,0:T(8,128)} %get-tuple-element.683), channel_id=1, source_target_pairs={{0,1},{1,2},{2,3},{3,4},{4,5},{5,6},{6,7},{8,9},{9,10},{10,11},{11... | collective-permute-start | bytes 1572872 | tf_op jit(solution)/shard_map/while/body/eval_jaxpr/ppermute | solution.py:17
  155.2 3.4 copy-start.5
  161.1 10.7 %collective-permute-start = (f32[2,2,1,256,128]{4,3,2,1,0:T(8,128)}, f32[2,2,1,256,128]{4,3,2,1,0:T(8,128)}, u32[]{:S(2)}, u32[]{:S(2)}) collective-permute-start(f32[2,2,1,256,128]{4,3,2,1,0:T(8,128)} %get-tuple-element.682), channel_id=1, source_target_pairs={{1,0},{2,1},{3,2},{4,3},{5,4},{6,5},{7,6},{9,8},{10,9},{11,10},{12... | collective-permute-start | bytes 1572872 | tf_op jit(solution)/shard_map/while/body/eval_jaxpr/ppermute | solution.py:20
  162.4 9.4 %collective-permute-start.1 = (f32[2,2,1,256,128]{4,3,2,1,0:T(8,128)}, f32[2,2,1,256,128]{4,3,2,1,0:T(8,128)}, u32[]{:S(2)}, u32[]{:S(2)}) collective-permute-start(f32[2,2,1,256,128]{4,3,2,1,0:T(8,128)} %get-tuple-element.683), channel_id=1, source_target_pairs={{0,1},{1,2},{2,3},{3,4},{4,5},{5,6},{6,7},{8,9},{9,10},{10,11},{11... | collective-permute-start | bytes 1572872 | tf_op jit(solution)/shard_map/while/body/eval_jaxpr/ppermute | solution.py:17
  173.9 3.4 copy-start.4
  173.9 3.4 copy-start.5
  179.9 10.7 %collective-permute-start = (f32[2,2,1,256,128]{4,3,2,1,0:T(8,128)}, f32[2,2,1,256,128]{4,3,2,1,0:T(8,128)}, u32[]{:S(2)}, u32[]{:S(2)}) collective-permute-start(f32[2,2,1,256,128]{4,3,2,1,0:T(8,128)} %get-tuple-element.682), channel_id=1, source_target_pairs={{1,0},{2,1},{3,2},{4,3},{5,4},{6,5},{7,6},{9,8},{10,9},{11,10},{12... | collective-permute-start | bytes 1572872 | tf_op jit(solution)/shard_map/while/body/eval_jaxpr/ppermute | solution.py:20
  181.2 9.4 %collective-permute-start.1 = (f32[2,2,1,256,128]{4,3,2,1,0:T(8,128)}, f32[2,2,1,256,128]{4,3,2,1,0:T(8,128)}, u32[]{:S(2)}, u32[]{:S(2)}) collective-permute-start(f32[2,2,1,256,128]{4,3,2,1,0:T(8,128)} %get-tuple-element.683), channel_id=1, source_target_pairs={{0,1},{1,2},{2,3},{3,4},{4,5},{5,6},{6,7},{8,9},{9,10},{10,11},{11... | collective-permute-start | bytes 1572872 | tf_op jit(solution)/shard_map/while/body/eval_jaxpr/ppermute | solution.py:17
  192.7 3.4 copy-start.4
  192.7 3.4 copy-start.5
  198.7 10.7 %collective-permute-start = (f32[2,2,1,256,128]{4,3,2,1,0:T(8,128)}, f32[2,2,1,256,128]{4,3,2,1,0:T(8,128)}, u32[]{:S(2)}, u32[]{:S(2)}) collective-permute-start(f32[2,2,1,256,128]{4,3,2,1,0:T(8,128)} %get-tuple-element.682), channel_id=1, source_target_pairs={{1,0},{2,1},{3,2},{4,3},{5,4},{6,5},{7,6},{9,8},{10,9},{11,10},{12... | collective-permute-start | bytes 1572872 | tf_op jit(solution)/shard_map/while/body/eval_jaxpr/ppermute | solution.py:20
  200.0 9.4 %collective-permute-start.1 = (f32[2,2,1,256,128]{4,3,2,1,0:T(8,128)}, f32[2,2,1,256,128]{4,3,2,1,0:T(8,128)}, u32[]{:S(2)}, u32[]{:S(2)}) collective-permute-start(f32[2,2,1,256,128]{4,3,2,1,0:T(8,128)} %get-tuple-element.683), channel_id=1, source_target_pairs={{0,1},{1,2},{2,3},{3,4},{4,5},{5,6},{6,7},{8,9},{9,10},{10,11},{11... | collective-permute-start | bytes 1572872 | tf_op jit(solution)/shard_map/while/body/eval_jaxpr/ppermute | solution.py:17
  211.5 3.4 copy-start.5
  217.5 10.7 %collective-permute-start = (f32[2,2,1,256,128]{4,3,2,1,0:T(8,128)}, f32[2,2,1,256,128]{4,3,2,1,0:T(8,128)}, u32[]{:S(2)}, u32[]{:S(2)}) collective-permute-start(f32[2,2,1,256,128]{4,3,2,1,0:T(8,128)} %get-tuple-element.682), channel_id=1, source_target_pairs={{1,0},{2,1},{3,2},{4,3},{5,4},{6,5},{7,6},{9,8},{10,9},{11,10},{12... | collective-permute-start | bytes 1572872 | tf_op jit(solution)/shard_map/while/body/eval_jaxpr/ppermute | solution.py:20
  218.7 9.4 %collective-permute-start.1 = (f32[2,2,1,256,128]{4,3,2,1,0:T(8,128)}, f32[2,2,1,256,128]{4,3,2,1,0:T(8,128)}, u32[]{:S(2)}, u32[]{:S(2)}) collective-permute-start(f32[2,2,1,256,128]{4,3,2,1,0:T(8,128)} %get-tuple-element.683), channel_id=1, source_target_pairs={{0,1},{1,2},{2,3},{3,4},{4,5},{5,6},{6,7},{8,9},{9,10},{10,11},{11... | collective-permute-start | bytes 1572872 | tf_op jit(solution)/shard_map/while/body/eval_jaxpr/ppermute | solution.py:17
  230.3 3.4 copy-start.4
  230.3 3.4 copy-start.5
  236.2 10.7 %collective-permute-start = (f32[2,2,1,256,128]{4,3,2,1,0:T(8,128)}, f32[2,2,1,256,128]{4,3,2,1,0:T(8,128)}, u32[]{:S(2)}, u32[]{:S(2)}) collective-permute-start(f32[2,2,1,256,128]{4,3,2,1,0:T(8,128)} %get-tuple-element.682), channel_id=1, source_target_pairs={{1,0},{2,1},{3,2},{4,3},{5,4},{6,5},{7,6},{9,8},{10,9},{11,10},{12... | collective-permute-start | bytes 1572872 | tf_op jit(solution)/shard_map/while/body/eval_jaxpr/ppermute | solution.py:20
  237.5 9.4 %collective-permute-start.1 = (f32[2,2,1,256,128]{4,3,2,1,0:T(8,128)}, f32[2,2,1,256,128]{4,3,2,1,0:T(8,128)}, u32[]{:S(2)}, u32[]{:S(2)}) collective-permute-start(f32[2,2,1,256,128]{4,3,2,1,0:T(8,128)} %get-tuple-element.683), channel_id=1, source_target_pairs={{0,1},{1,2},{2,3},{3,4},{4,5},{5,6},{6,7},{8,9},{9,10},{10,11},{11... | collective-permute-start | bytes 1572872 | tf_op jit(solution)/shard_map/while/body/eval_jaxpr/ppermute | solution.py:17
  249.1 3.4 copy-start.5
  255.0 10.7 %collective-permute-start = (f32[2,2,1,256,128]{4,3,2,1,0:T(8,128)}, f32[2,2,1,256,128]{4,3,2,1,0:T(8,128)}, u32[]{:S(2)}, u32[]{:S(2)}) collective-permute-start(f32[2,2,1,256,128]{4,3,2,1,0:T(8,128)} %get-tuple-element.682), channel_id=1, source_target_pairs={{1,0},{2,1},{3,2},{4,3},{5,4},{6,5},{7,6},{9,8},{10,9},{11,10},{12... | collective-permute-start | bytes 1572872 | tf_op jit(solution)/shard_map/while/body/eval_jaxpr/ppermute | solution.py:20
  256.3 9.4 %collective-permute-start.1 = (f32[2,2,1,256,128]{4,3,2,1,0:T(8,128)}, f32[2,2,1,256,128]{4,3,2,1,0:T(8,128)}, u32[]{:S(2)}, u32[]{:S(2)}) collective-permute-start(f32[2,2,1,256,128]{4,3,2,1,0:T(8,128)} %get-tuple-element.683), channel_id=1, source_target_pairs={{0,1},{1,2},{2,3},{3,4},{4,5},{5,6},{6,7},{8,9},{9,10},{10,11},{11... | collective-permute-start | bytes 1572872 | tf_op jit(solution)/shard_map/while/body/eval_jaxpr/ppermute | solution.py:17
  267.8 3.4 copy-start.5
  273.8 10.7 %collective-permute-start = (f32[2,2,1,256,128]{4,3,2,1,0:T(8,128)}, f32[2,2,1,256,128]{4,3,2,1,0:T(8,128)}, u32[]{:S(2)}, u32[]{:S(2)}) collective-permute-start(f32[2,2,1,256,128]{4,3,2,1,0:T(8,128)} %get-tuple-element.682), channel_id=1, source_target_pairs={{1,0},{2,1},{3,2},{4,3},{5,4},{6,5},{7,6},{9,8},{10,9},{11,10},{12... | collective-permute-start | bytes 1572872 | tf_op jit(solution)/shard_map/while/body/eval_jaxpr/ppermute | solution.py:20
  275.1 9.4 %collective-permute-start.1 = (f32[2,2,1,256,128]{4,3,2,1,0:T(8,128)}, f32[2,2,1,256,128]{4,3,2,1,0:T(8,128)}, u32[]{:S(2)}, u32[]{:S(2)}) collective-permute-start(f32[2,2,1,256,128]{4,3,2,1,0:T(8,128)} %get-tuple-element.683), channel_id=1, source_target_pairs={{0,1},{1,2},{2,3},{3,4},{4,5},{5,6},{6,7},{8,9},{9,10},{10,11},{11... | collective-permute-start | bytes 1572872 | tf_op jit(solution)/shard_map/while/body/eval_jaxpr/ppermute | solution.py:17
  286.6 3.4 copy-start.5
  292.6 10.7 %collective-permute-start = (f32[2,2,1,256,128]{4,3,2,1,0:T(8,128)}, f32[2,2,1,256,128]{4,3,2,1,0:T(8,128)}, u32[]{:S(2)}, u32[]{:S(2)}) collective-permute-start(f32[2,2,1,256,128]{4,3,2,1,0:T(8,128)} %get-tuple-element.682), channel_id=1, source_target_pairs={{1,0},{2,1},{3,2},{4,3},{5,4},{6,5},{7,6},{9,8},{10,9},{11,10},{12... | collective-permute-start | bytes 1572872 | tf_op jit(solution)/shard_map/while/body/eval_jaxpr/ppermute | solution.py:20
  293.9 9.4 %collective-permute-start.1 = (f32[2,2,1,256,128]{4,3,2,1,0:T(8,128)}, f32[2,2,1,256,128]{4,3,2,1,0:T(8,128)}, u32[]{:S(2)}, u32[]{:S(2)}) collective-permute-start(f32[2,2,1,256,128]{4,3,2,1,0:T(8,128)} %get-tuple-element.683), channel_id=1, source_target_pairs={{0,1},{1,2},{2,3},{3,4},{4,5},{5,6},{6,7},{8,9},{9,10},{10,11},{11... | collective-permute-start | bytes 1572872 | tf_op jit(solution)/shard_map/while/body/eval_jaxpr/ppermute | solution.py:17
  305.4 3.4 copy-start.5
  311.4 10.7 %collective-permute-start = (f32[2,2,1,256,128]{4,3,2,1,0:T(8,128)}, f32[2,2,1,256,128]{4,3,2,1,0:T(8,128)}, u32[]{:S(2)}, u32[]{:S(2)}) collective-permute-start(f32[2,2,1,256,128]{4,3,2,1,0:T(8,128)} %get-tuple-element.682), channel_id=1, source_target_pairs={{1,0},{2,1},{3,2},{4,3},{5,4},{6,5},{7,6},{9,8},{10,9},{11,10},{12... | collective-permute-start | bytes 1572872 | tf_op jit(solution)/shard_map/while/body/eval_jaxpr/ppermute | solution.py:20
  312.6 9.4 %collective-permute-start.1 = (f32[2,2,1,256,128]{4,3,2,1,0:T(8,128)}, f32[2,2,1,256,128]{4,3,2,1,0:T(8,128)}, u32[]{:S(2)}, u32[]{:S(2)}) collective-permute-start(f32[2,2,1,256,128]{4,3,2,1,0:T(8,128)} %get-tuple-element.683), channel_id=1, source_target_pairs={{0,1},{1,2},{2,3},{3,4},{4,5},{5,6},{6,7},{8,9},{9,10},{10,11},{11... | collective-permute-start | bytes 1572872 | tf_op jit(solution)/shard_map/while/body/eval_jaxpr/ppermute | solution.py:17
  324.2 3.4 copy-start.5
  331.7 28.8 %all-to-all-start.2 = ((f32[2,2,4,256,128]{4,2,1,0,3:T(4,128)}), f32[2,2,4,256,128]{4,2,1,0,3:T(4,128)S(1)}, u32[]{:S(2)}, u32[]{:S(2)}) async-start(f32[2,2,4,256,128]{4,2,1,0,3:T(4,128)} %copy.66), calls=%async_computation.2 | async-start | bytes 4194304 | tf_op jit(solution)/shard_map/all_to_all | solution.py:166
  369.3 29.8 %all-to-all-start.3 = ((f32[8,2,4,64,128]{4,3,2,1,0:T(8,128)}), f32[8,2,4,64,128]{4,3,2,1,0:T(8,128)S(1)}, u32[]{:S(2)}, u32[]{:S(2)}) async-start(f32[8,2,4,64,128]{4,3,2,1,0:T(8,128)} %copy.69), calls=%async_computation.3 | async-start | bytes 4194304 | tf_op jit(solution)/shard_map/all_to_all | solution.py:167
  (101 other events, 244.5 us)
